TPU v7x, 32 devices: a whole 2x2x4 slice. The times are simulated.
32 devices in a mesh: ctx: 16 (over z, y, x), tp: 2 (over core).
Axes of the slice: x: 2, y: 2, z: 4, core: 2. Of those that a mesh axis runs over, the one named last changes fastest.
Arguments:
- queries: bfloat16 [2048, 4096], P('ctx', 'tp'), may hold values from -220 to 220
- keys: bfloat16 [2048, 1024], P('ctx', 'tp'), may hold values from -6 to 6
- values: bfloat16 [2048, 1024], P('ctx', 'tp'), may hold values from -6 to 6
- out_weight: bfloat16 [4096, 4096], P('tp'), may hold values from -0.09375 to 0.09375
- residual: bfloat16 [2048, 4096], P('ctx', 'tp'), may hold values from -1.5 to 1.5
- norm_gain: bfloat16 [4096], P('tp'), may hold values from 0.5 to 1.5
- span_order: int32 [32], replicated, may hold values from 0 to 31, as said below
Outputs:
- normed: bfloat16 [2048, 4096], P('ctx', 'tp')
Inputs may be any that keep to these rules, and one draw needn't show every extreme that they name: `span_order`: every span appears in exactly one slot. The two slots of one index d of ctx (slots 2d and 2d + 1) hold a span p and its mirror, the span at the same place counted from the end of the sequence; which index holds which pair, and the order of the two, are drawn.
All inputs are finite; a program needn't handle non-finite values.
Results may differ from a plain program's by a relative error of at most 0.009.
Values may be sent and summed in bfloat16 or wider, within the bound.
A program may use at most 64 MiB of HBM per device.

v0:
```python
import math
import jax
import jax.numpy as jnp
from jax import lax
from jax.sharding import PartitionSpec as P

D = 4096
HEAD_SIZE = 128
EPSILON = 1e-05


def per_device(queries, keys, values, out_weight, residual, norm_gain, span_order):
    local_rows = queries.shape[0]
    span_rows = local_rows // 2
    heads = queries.shape[1] // HEAD_SIZE
    kv_heads = keys.shape[1] // HEAD_SIZE
    group_size = heads // kv_heads
    scale = 1.0 / math.sqrt(HEAD_SIZE)
    device = lax.axis_index("ctx")
    owned = lax.dynamic_slice_in_dim(span_order, 2 * device, 2)
    offsets = jnp.arange(span_rows, dtype=jnp.int32)
    query_pos = (owned[:, None] * span_rows + offsets[None, :]).reshape(local_rows)
    query_mat = queries.reshape(local_rows, kv_heads, group_size, HEAD_SIZE)
    fresh = (
        jnp.full((kv_heads, group_size, local_rows), -1e30, jnp.float32),
        jnp.zeros((kv_heads, group_size, local_rows), jnp.float32),
        jnp.zeros((kv_heads, group_size, local_rows, HEAD_SIZE), jnp.float32),
    )
    carry = fresh
    key_piece = lax.all_gather(keys, "ctx", axis=0, tiled=True)
    value_piece = lax.all_gather(values, "ctx", axis=0, tiled=True)
    count = key_piece.shape[0]
    spans = count // span_rows
    per_step = max(1, min(spans, 1024 // span_rows))
    while spans % per_step != 0:
        per_step = per_step - 1
    steps = spans // per_step
    block_rows = per_step * span_rows
    key_pos_all = (span_order[:, None] * span_rows + offsets[None, :]).reshape(steps, block_rows)
    key_blocks = key_piece.reshape(steps, block_rows, kv_heads, HEAD_SIZE)
    value_blocks = value_piece.reshape(steps, block_rows, kv_heads, HEAD_SIZE)

    def scan_step(state, item):
        running, total, accum = state
        key_pos, key_mat, value_mat = item
        scores = (
            jnp.einsum("qhgd,khd->hgqk", query_mat, key_mat, preferred_element_type=jnp.float32)
            * scale
        )
        allowed = (key_pos[None, :] <= query_pos[:, None])[None, None, :, :]
        scores = jnp.where(allowed, scores, -1e30)
        newmax = jnp.maximum(running, jnp.max(scores, axis=-1))
        weights = jnp.where(allowed, jnp.exp(scores - newmax[..., None]), 0.0)
        fade = jnp.exp(running - newmax)
        total = total * fade + jnp.sum(weights, axis=-1)
        accum = accum * fade[..., None] + jnp.einsum(
            "hgqk,khd->hgqd",
            weights.astype(jnp.bfloat16),
            value_mat,
            preferred_element_type=jnp.float32,
        )
        return ((newmax, total, accum), None)

    carry, unused = lax.scan(scan_step, carry, (key_pos_all, key_blocks, value_blocks))
    running, total, accum = carry
    attended = accum / total[..., None]
    attended = (
        jnp.transpose(attended, (2, 0, 1, 3))
        .reshape(local_rows, heads * HEAD_SIZE)
        .astype(jnp.bfloat16)
    )
    partial_value = jnp.dot(attended, out_weight, preferred_element_type=jnp.float32)
    share = lax.psum_scatter(
        partial_value.astype(jnp.bfloat16), "tp", scatter_dimension=1, tiled=True
    ).astype(jnp.float32)
    hidden = (residual.astype(jnp.float32) + share).astype(jnp.bfloat16)
    hidden_f = hidden.astype(jnp.float32)
    squares = lax.psum(jnp.sum(hidden_f * hidden_f, axis=1), "tp")
    factor = lax.rsqrt(squares / D + EPSILON)
    normed = hidden_f * factor[:, None] * norm_gain.astype(jnp.float32)[None, :]
    return normed.astype(jnp.bfloat16)


def solution(mesh):
    return jax.shard_map(
        per_device,
        mesh=mesh,
        in_specs=(
            P("ctx", "tp"),
            P("ctx", "tp"),
            P("ctx", "tp"),
            P("tp", None),
            P("ctx", "tp"),
            P("tp"),
            P(),
        ),
        out_specs=P("ctx", "tp"),
        check_vma=False,
    )
```

profile of v0, /device:TPU:0, one launch (start us, length us, event | category | flops | bytes accessed | tf_op | source)
XLA Modules:
  0.0 206.1 jit_solution(13089571367657228611)
XLA Ops:
  6.5 0.0 all-gather.3.cloned.1.call-start
  6.5 0.7 all-gather.3.cloned.1.call-update
  7.3 0.0 all-gather.5.cloned.1.call-start
  7.3 0.7 all-gather.5.cloned.1.call-update
  8.0 0.0 reduce-scatter.2.cloned.1.call-start
  8.1 1.3 copy.10
  9.4 1.0 copy.12
  10.4 0.7 broadcast_multiply_fusion
  11.1 0.1 add.60
  11.2 0.1 add.61
  11.2 0.1 add.62
  11.3 0.1 add.64
  11.4 0.7 dynamic-slice_multiply_fusion
  12.1 61.1 %all-gather.3.cloned.1.call-done = bf16[2048,512]{1,0:T(8,128)(2,1)} async-done(((bf16[128,512]{1,0:T(8,128)(2,1)}), bf16[2048,512]{1,0:T(8,128)(2,1)}) %all-gather.3.cloned.1.call-update) | async-done | bytes 2097168 | tf_op jit(solution)/shard_map/all_gather | solution.py:30
  73.2 2.5 %reshape.56 = bf16[2,1024,4,128]{3,2,1,0:T(4,128)(2,1)S(1)} reshape(bf16[2048,512]{1,0:T(8,128)(2,1)} %all-gather.3.cloned.1.call-done) | data formatting | bytes 4194304 | tf_op jit(solution)/shard_map/reshape | solution.py:40
  75.8 59.4 %all-gather.5.cloned.1.call-done = bf16[2048,512]{1,0:T(8,128)(2,1)} async-done(((bf16[128,512]{1,0:T(8,128)(2,1)}), bf16[2048,512]{1,0:T(8,128)(2,1)}) %all-gather.5.cloned.1.call-update) | async-done | bytes 2097168 | tf_op jit(solution)/shard_map/all_gather | solution.py:31
  135.2 4.0 %reshape.58 = bf16[2,1024,4,128]{3,2,1,0:T(4,128)(2,1)} reshape(bf16[2048,512]{1,0:T(8,128)(2,1)} %all-gather.5.cloned.1.call-done) | data formatting | bytes 4194304 | tf_op jit(solution)/shard_map/reshape | solution.py:41
  139.2 36.3 %while.15 = (s32[]{:T(128)}, f32[4,4,128]{2,1,0:T(4,128)S(1)}, f32[4,4,128]{2,1,0:T(4,128)S(1)}, f32[4,4,128,128]{3,2,1,0:T(8,128)}, s32[2,1024]{1,0:T(2,128)S(1...) while((s32[]{:T(128)}, f32[4,4,128]{2,1,0:T(4,128)S(1)}, ...), condition=%wide.region_3.4_spmd.clone, body=%wide.region_0.3_spmd.clone.sunk | while | flops 1101932672 | bytes 68303016 | solution.py:64
  139.2 0.1 iota_add_fusion.2
  139.3 0.1 le.33
  139.4 0.2 broadcast_compare_fusion.2
  139.6 2.0 constant_dynamic-slice_fusion.6
  141.6 5.6 %fusion.30 = (f32[4,4,128]{2,1,0:T(4,128)S(1)}, f32[4,1024,128,4]{2,1,3,0:T(8,128)}) fusion(pred[128,1024]{0,1:T(8,128)(4,1)S(1)} %broadcast_compare_fusion.2, bf16[128,4,4,128]{3,0,2,1:T(8,128)(2,1)} %get-tuple-element.216, bf16[1,1024,4,128]{3,2,1,0:T(4,128)(2,1)S(1)} %get-tuple-element.182), kind=kOutput, calls=%fused_computation.3.clone.1 | convolution fusion | flops 543160320 | bytes 10100736 | tf_op jit(solution)/shard_map/while/body/eval_jaxpr/qhgd,khd->hgqk/dot_general | solution.py:47
  147.2 0.0 copy-start
  147.2 4.6 %fusion.31 = f32[4,4,128]{2,1,0:T(4,128)S(1)} fusion(f32[4,1024,128,4]{2,1,3,0:T(8,128)} %get-tuple-element.184, f32[4,4,128]{2,1,0:T(4,128)S(1)} %select_maximum_fusion.2, pred[128,1024]{0,1:T(8,128)(4,1)S(1)} %broadcast_compare_fusion.2), kind=kLoop, calls=%fused_computation.5.clone.1 | loop fusion | flops 10483712 | bytes 8536064 | tf_op jit(solution)/shard_map/while/body/eval_jaxpr/reduce_sum | solution.py:55
  151.8 1.2 copy-done
  153.0 3.8 %fusion.33 = f32[4,4,128,128]{3,2,1,0:T(8,128)} fusion(f32[4,1024,128,4]{2,1,3,0:T(8,128)S(1)} %copy-done, f32[4,4,128]{2,1,0:T(4,128)S(1)} %select_maximum_fusion.2, pred[128,1024]{0,1:T(8,128)(4,1)S(1)} %broadcast_compare_fusion.2, bf16[1,1024,4,128]{3,2,1,0:T(4,128)(2,1)S(1)} %get-tuple-element.186, f32[4,4,128,128]{3,2,1,0:T(8,128)} %get-tuple-element.202, ...), kind=kOutput, calls=%fused_computation.8.clone.1 | convolution fusion | flops 548143104 | bytes 11681793 | tf_op jit(solution)/shard_map/while/body/eval_jaxpr/hgqk,khd->hgqd/dot_general | solution.py:56
  156.8 0.1 iota_add_fusion.2
  156.9 0.1 le.33
  157.0 0.2 broadcast_compare_fusion.2
  157.2 2.0 constant_dynamic-slice_fusion.6
  159.2 5.6 %fusion.30 = (f32[4,4,128]{2,1,0:T(4,128)S(1)}, f32[4,1024,128,4]{2,1,3,0:T(8,128)}) fusion(pred[128,1024]{0,1:T(8,128)(4,1)S(1)} %broadcast_compare_fusion.2, bf16[128,4,4,128]{3,0,2,1:T(8,128)(2,1)} %get-tuple-element.216, bf16[1,1024,4,128]{3,2,1,0:T(4,128)(2,1)S(1)} %get-tuple-element.182), kind=kOutput, calls=%fused_computation.3.clone.1 | convolution fusion | flops 543160320 | bytes 10100736 | tf_op jit(solution)/shard_map/while/body/eval_jaxpr/qhgd,khd->hgqk/dot_general | solution.py:47
  164.8 0.0 copy-start
  164.8 4.6 %fusion.31 = f32[4,4,128]{2,1,0:T(4,128)S(1)} fusion(f32[4,1024,128,4]{2,1,3,0:T(8,128)} %get-tuple-element.184, f32[4,4,128]{2,1,0:T(4,128)S(1)} %select_maximum_fusion.2, pred[128,1024]{0,1:T(8,128)(4,1)S(1)} %broadcast_compare_fusion.2), kind=kLoop, calls=%fused_computation.5.clone.1 | loop fusion | flops 10483712 | bytes 8536064 | tf_op jit(solution)/shard_map/while/body/eval_jaxpr/reduce_sum | solution.py:55
  169.5 1.2 copy-done
  170.6 4.8 %fusion.33 = f32[4,4,128,128]{3,2,1,0:T(8,128)} fusion(f32[4,1024,128,4]{2,1,3,0:T(8,128)S(1)} %copy-done, f32[4,4,128]{2,1,0:T(4,128)S(1)} %select_maximum_fusion.2, pred[128,1024]{0,1:T(8,128)(4,1)S(1)} %broadcast_compare_fusion.2, bf16[1,1024,4,128]{3,2,1,0:T(4,128)(2,1)S(1)} %get-tuple-element.186, f32[4,4,128,128]{3,2,1,0:T(8,128)} %get-tuple-element.202, ...), kind=kOutput, calls=%fused_computation.8.clone.1 | convolution fusion | flops 548143104 | bytes 11681793 | tf_op jit(solution)/shard_map/while/body/eval_jaxpr/hgqk,khd->hgqd/dot_general | solution.py:56
  175.5 1.6 copy.14
  177.0 0.1 divide_convert_fusion
  177.2 0.0 copy-start.2
  177.2 0.0 copy-start.1
  177.2 9.2 %convolution_convert_fusion = bf16[128,4096]{1,0:T(8,128)(2,1)} fusion(bf16[128,2048]{0,1:T(8,128)(2,1)S(1)} %bitcast.49, bf16[2048,4096]{1,0:T(8,128)(2,1)} %param.12), kind=kOutput, calls=%fused_computation.25 | convolution fusion | flops 2148007936 | bytes 18350080 | tf_op jit(solution)/shard_map/dot_general | solution.py:72
  186.4 0.0 reduce-scatter.2.cloned.1.call-update
  186.4 0.0 copy-done.2
  186.4 7.3 %reduce-scatter.2.cloned.1.call-done = bf16[128,2048]{1,0:T(8,128)(2,1)} async-done(((bf16[128,4096]{1,0:T(8,128)(2,1)}), bf16[128,2048]{1,0:T(8,128)(2,1)}) %reduce-scatter.2.cloned.1.call-update) | async-done | bytes 524304 | tf_op jit(solution)/shard_map/reduce_scatter | solution.py:73
  193.8 0.0 copy-done.1
  193.8 1.3 fusion.16
  195.1 2.5 %psum.7 = f32[128]{0:T(128)S(1)} all-reduce(f32[128]{0:T(128)S(1)} %fusion.16), channel_id=1, replica_groups=mesh['ctx'=16,'tp'=2] {'tp'}, use_global_device_ids=true, to_apply=%region_6.7 | all-reduce | flops 128 | bytes 1024 | tf_op jit(solution)/shard_map/psum | solution.py:78
  197.5 2.0 fusion.18
  (15 shorter events, 0.1 us)
Async XLA Ops:
  6.5 66.7 %all-gather.3.cloned.1.call-start = ((), (), s32[]{:S(2)}) async-start(), calls=%async_computation.1 | async-start | bytes 2228224 | tf_op jit(solution)/shard_map/all_gather | solution.py:30
  7.3 128.0 %all-gather.5.cloned.1.call-start = ((), (), s32[]{:S(2)}) async-start(), calls=%async_computation.2 | async-start | bytes 2228224 | tf_op jit(solution)/shard_map/all_gather | solution.py:31
  8.0 185.7 %reduce-scatter.2.cloned.1.call-start = ((), (), s32[]{:S(2)}) async-start(), calls=%async_computation.3 | async-start | bytes 1572864 | tf_op jit(solution)/shard_map/reduce_scatter | solution.py:73
  147.2 5.8 %copy-start = (f32[4,1024,128,4]{2,1,3,0:T(8,128)S(1)}, f32[4,1024,128,4]{2,1,3,0:T(8,128)}, u32[]{:S(2)}) copy-start(f32[4,1024,128,4]{2,1,3,0:T(8,128)} %get-tuple-element.184) | copy-start | bytes 25165828 | tf_op jit(solution)/shard_map/while
  164.8 5.8 %copy-start = (f32[4,1024,128,4]{2,1,3,0:T(8,128)S(1)}, f32[4,1024,128,4]{2,1,3,0:T(8,128)}, u32[]{:S(2)}) copy-start(f32[4,1024,128,4]{2,1,3,0:T(8,128)} %get-tuple-element.184) | copy-start | bytes 25165828 | tf_op jit(solution)/shard_map/while
  177.2 9.2 %copy-start.2 = (bf16[2048]{0:T(1024)(128)(2,1)S(1)}, bf16[2048]{0:T(1024)(128)(2,1)}, u32[]{:S(2)}) copy-start(bf16[2048]{0:T(1024)(128)(2,1)} %param.14) | copy-start | bytes 12292
  177.2 16.6 %copy-start.1 = (bf16[128,2048]{1,0:T(8,128)(2,1)S(1)}, bf16[128,2048]{1,0:T(8,128)(2,1)}, u32[]{:S(2)}) copy-start(bf16[128,2048]{1,0:T(8,128)(2,1)} %param.13) | copy-start | bytes 1572868
Sparse Core Ops, SparseCore 0:
  10.1 63.0 all-gather.2
  76.0 59.1 all-gather.4
  186.5 7.1 reduce-scatter.1
where the time goes:
time: 207 us; the launch traced here: 206 us
  waiting for transfers between devices  129 us (62%)
  matrix products  29.1 us (14%)
  local copies, waits for them, and re-layouts  17.2 us (8%)
  other arithmetic  14.7 us (7%)
  between operations  13.2 us (6%)
  blocking collectives  2.46 us (1%)
    all_gather x1, waiting for transfers between devices, per_device(): key_piece = lax.all_gather(keys, 'ctx', axis=0, tiled=True)  61.1 us
    all_gather x1, waiting for transfers between devices, per_device(): value_piece = lax.all_gather(values, 'ctx', axis=0, tiled=True)  59.4 us
    dot_general x2, matrix products, scan_step(): jnp.einsum('qhgd,khd->hgqk', query_mat, key_mat, preferred_element_type=j...  11.3 us
    reduce_sum x2, other arithmetic, scan_step(): total = total * fade + jnp.sum(weights, axis=-1)  9.21 us
    dot_general x1, matrix products, per_device(): jnp.dot(attended, out_weight, preferred_element_type=jnp.float32)  9.19 us
    dot_general x2, matrix products, scan_step(): jnp.einsum('hgqk,khd->hgqd', weights.astype(jnp.bfloat16), value_mat, pre...  8.61 us
    reduce_scatter x1, waiting for transfers between devices, per_device(): lax.psum_scatter(partial_value.astype(jnp.bfloat16), 'tp', scatter_dimens...  7.33 us
  transfers between devices with their start and end apart: 3, of which 3 were waited for; matrix products, arithmetic and copies ran while one was open for 3% of the time, Pallas kernels for 0%

commit v1 on v0

--- a/solution.py
+++ b/solution.py
@@ -28,7 +28,17 @@
     )
     carry = fresh
     key_piece = lax.all_gather(keys, "ctx", axis=0, tiled=True)
-    value_piece = lax.all_gather(values, "ctx", axis=0, tiled=True)
+    found = []
+    dev_n = lax.axis_size("ctx")
+    for b in tuple(range(dev_n)):
+        found.append((b, (b + 1) % dev_n))
+    local_now = [None] * dev_n
+    local_now[dev_n - 1] = values
+    for s in range(dev_n - 2, -1, -1):
+        local_now[s] = lax.ppermute(local_now[s + 1], "ctx", found)
+    value_piece = jnp.roll(
+        jnp.concatenate(local_now, axis=0), (lax.axis_index("ctx") + 1) * values.shape[0], axis=0
+    )
     count = key_piece.shape[0]
     spans = count // span_rows
     per_step = max(1, min(spans, 1024 // span_rows))

time: 207 us -> 246 us (1.19)
  waiting for transfers between devices: 129 us -> 165 us
  starting transfers between devices: 0.08 us -> 3.05 us
    ppermute x0 -> x15, waiting for transfers between devices: none -> 127 us  [per_device(): local_now[s] = lax.ppermute(local_now[s + 1], 'ctx', found)]
    all_gather x1 -> x0, waiting for transfers between devices: 59.4 us -> none  [per_device(): value_piece = lax.all_gather(values, 'ctx', axis=0, tiled=True)]
    all_gather x1, waiting for transfers between devices: 61.1 us -> 31.1 us  [per_device(): key_piece = lax.all_gather(keys, 'ctx', axis=0, tiled=True)]
    ppermute x0 -> x15, starting transfers between devices: none -> 3 us  [per_device(): local_now[s] = lax.ppermute(local_now[s + 1], 'ctx', found)]
  transfers between devices with their start and end apart: 3 -> 17, of which waited for: 3 -> 17; matrix products, arithmetic and copies ran while one was open for 3% -> 3% of each run, Pallas kernels for 0% -> 0%
where the time goes in v1:
time: 246 us
  waiting for transfers between devices  165 us (67%)
  matrix products  27 us (11%)
  local copies, waits for them, and re-layouts  19.1 us (8%)
  other arithmetic  14.7 us (6%)
  between operations  13.8 us (6%)
  starting transfers between devices  3.05 us (1%)
  blocking collectives  2.46 us (1%)
    ppermute x15, waiting for transfers between devices, per_device(): local_now[s] = lax.ppermute(local_now[s + 1], 'ctx', found)  127 us
    all_gather x1, waiting for transfers between devices, per_device(): key_piece = lax.all_gather(keys, 'ctx', axis=0, tiled=True)  31.1 us
    reduce_sum x2, other arithmetic, scan_step(): total = total * fade + jnp.sum(weights, axis=-1)  9.21 us
    dot_general x2, matrix products, scan_step(): jnp.einsum('qhgd,khd->hgqk', query_mat, key_mat, preferred_element_type=j...  9.21 us
    dot_general x1, matrix products, per_device(): jnp.dot(attended, out_weight, preferred_element_type=jnp.float32)  9.2 us
    dot_general x2, matrix products, scan_step(): jnp.einsum('hgqk,khd->hgqd', weights.astype(jnp.bfloat16), value_mat, pre...  8.61 us
    reduce_scatter x1, waiting for transfers between devices, per_device(): lax.psum_scatter(partial_value.astype(jnp.bfloat16), 'tp', scatter_dimens...  7.33 us
  transfers between devices with their start and end apart: 17, of which 17 were waited for; matrix products, arithmetic and copies ran while one was open for 3% of the time, Pallas kernels for 0%

profile of v1, /device:TPU:0, one launch (start us, length us, event | category | flops | bytes accessed | tf_op | source)
XLA Modules:
  0.0 245.6 jit_solution(11424971565221419289)
XLA Ops:
  6.5 3.0 %collective-permute-start = (bf16[128,512]{1,0:T(8,128)(2,1)}, bf16[128,512]{1,0:T(8,128)(2,1)S(1)}, u32[]{:S(2)}, u32[]{:S(2)}) collective-permute-start(bf16[128,512]{1,0:T(8,128)(2,1)} %param.11), channel_id=1, source_target_pairs={{0,2},{2,4},{4,6},{6,8},{8,10},{10,12},{12,14},{14,16},{16,18},{18... | collective-permute-start | bytes 393224 | tf_op jit(solution)/shard_map/ppermute | solution.py:38
  9.5 7.8 %collective-permute-done = bf16[128,512]{1,0:T(8,128)(2,1)S(1)} collective-permute-done((bf16[128,512]{1,0:T(8,128)(2,1)}, bf16[128,512]{1,0:T(8,128)(2,1)S(1)}, u32[]{:S(2)}, u32[]{:S(2)}) %collective-permute-start) | collective-permute-done | bytes 131104 | tf_op jit(solution)/shard_map/ppermute | solution.py:38
  17.3 8.6 %collective-permute-done.1 = bf16[128,512]{1,0:T(8,128)(2,1)S(1)} collective-permute-done((bf16[128,512]{1,0:T(8,128)(2,1)S(1)}, bf16[128,512]{1,0:T(8,128)(2,1)S(1)}, u32[]{:S(2)}, u32[]{:S(2)}) %collective-permute-start.1) | collective-permute-done | bytes 131104 | tf_op jit(solution)/shard_map/ppermute | solution.py:38
  25.8 8.6 %collective-permute-done.2 = bf16[128,512]{1,0:T(8,128)(2,1)S(1)} collective-permute-done((bf16[128,512]{1,0:T(8,128)(2,1)S(1)}, bf16[128,512]{1,0:T(8,128)(2,1)S(1)}, u32[]{:S(2)}, u32[]{:S(2)}) %collective-permute-start.2) | collective-permute-done | bytes 131104 | tf_op jit(solution)/shard_map/ppermute | solution.py:38
  34.4 8.6 %collective-permute-done.3 = bf16[128,512]{1,0:T(8,128)(2,1)S(1)} collective-permute-done((bf16[128,512]{1,0:T(8,128)(2,1)S(1)}, bf16[128,512]{1,0:T(8,128)(2,1)S(1)}, u32[]{:S(2)}, u32[]{:S(2)}) %collective-permute-start.3) | collective-permute-done | bytes 131104 | tf_op jit(solution)/shard_map/ppermute | solution.py:38
  43.0 8.6 %collective-permute-done.4 = bf16[128,512]{1,0:T(8,128)(2,1)S(1)} collective-permute-done((bf16[128,512]{1,0:T(8,128)(2,1)S(1)}, bf16[128,512]{1,0:T(8,128)(2,1)S(1)}, u32[]{:S(2)}, u32[]{:S(2)}) %collective-permute-start.4) | collective-permute-done | bytes 131104 | tf_op jit(solution)/shard_map/ppermute | solution.py:38
  51.5 8.9 %collective-permute-done.5 = bf16[128,512]{1,0:T(8,128)(2,1)S(1)} collective-permute-done((bf16[128,512]{1,0:T(8,128)(2,1)S(1)}, bf16[128,512]{1,0:T(8,128)(2,1)S(1)}, u32[]{:S(2)}, u32[]{:S(2)}) %collective-permute-start.5) | collective-permute-done | bytes 131104 | tf_op jit(solution)/shard_map/ppermute | solution.py:38
  60.4 9.9 %collective-permute-done.6 = bf16[128,512]{1,0:T(8,128)(2,1)S(1)} collective-permute-done((bf16[128,512]{1,0:T(8,128)(2,1)S(1)}, bf16[128,512]{1,0:T(8,128)(2,1)S(1)}, u32[]{:S(2)}, u32[]{:S(2)}) %collective-permute-start.6) | collective-permute-done | bytes 131104 | tf_op jit(solution)/shard_map/ppermute | solution.py:38
  70.3 9.1 %collective-permute-done.7 = bf16[128,512]{1,0:T(8,128)(2,1)S(1)} collective-permute-done((bf16[128,512]{1,0:T(8,128)(2,1)S(1)}, bf16[128,512]{1,0:T(8,128)(2,1)S(1)}, u32[]{:S(2)}, u32[]{:S(2)}) %collective-permute-start.7) | collective-permute-done | bytes 131104 | tf_op jit(solution)/shard_map/ppermute | solution.py:38
  79.4 8.6 %collective-permute-done.8 = bf16[128,512]{1,0:T(8,128)(2,1)S(1)} collective-permute-done((bf16[128,512]{1,0:T(8,128)(2,1)S(1)}, bf16[128,512]{1,0:T(8,128)(2,1)S(1)}, u32[]{:S(2)}, u32[]{:S(2)}) %collective-permute-start.8) | collective-permute-done | bytes 131104 | tf_op jit(solution)/shard_map/ppermute | solution.py:38
  88.0 8.6 %collective-permute-done.9 = bf16[128,512]{1,0:T(8,128)(2,1)S(1)} collective-permute-done((bf16[128,512]{1,0:T(8,128)(2,1)S(1)}, bf16[128,512]{1,0:T(8,128)(2,1)S(1)}, u32[]{:S(2)}, u32[]{:S(2)}) %collective-permute-start.9) | collective-permute-done | bytes 131104 | tf_op jit(solution)/shard_map/ppermute | solution.py:38
  96.5 8.6 %collective-permute-done.10 = bf16[128,512]{1,0:T(8,128)(2,1)S(1)} collective-permute-done((bf16[128,512]{1,0:T(8,128)(2,1)S(1)}, bf16[128,512]{1,0:T(8,128)(2,1)S(1)}, u32[]{:S(2)}, u32[]{:S(2)}) %collective-permute-start.10) | collective-permute-done | bytes 131104 | tf_op jit(solution)/shard_map/ppermute | solution.py:38
  105.1 8.6 %collective-permute-done.11 = bf16[128,512]{1,0:T(8,128)(2,1)S(1)} collective-permute-done((bf16[128,512]{1,0:T(8,128)(2,1)S(1)}, bf16[128,512]{1,0:T(8,128)(2,1)S(1)}, u32[]{:S(2)}, u32[]{:S(2)}) %collective-permute-start.11) | collective-permute-done | bytes 131104 | tf_op jit(solution)/shard_map/ppermute | solution.py:38
  113.7 8.8 %collective-permute-done.12 = bf16[128,512]{1,0:T(8,128)(2,1)S(1)} collective-permute-done((bf16[128,512]{1,0:T(8,128)(2,1)S(1)}, bf16[128,512]{1,0:T(8,128)(2,1)S(1)}, u32[]{:S(2)}, u32[]{:S(2)}) %collective-permute-start.12) | collective-permute-done | bytes 131104 | tf_op jit(solution)/shard_map/ppermute | solution.py:38
  122.6 0.7 broadcast_multiply_fusion
  123.2 0.1 add.73
  123.4 0.1 add.75
  123.5 8.6 %collective-permute-done.13 = bf16[128,512]{1,0:T(8,128)(2,1)S(1)} collective-permute-done((bf16[128,512]{1,0:T(8,128)(2,1)S(1)}, bf16[128,512]{1,0:T(8,128)(2,1)S(1)}, u32[]{:S(2)}, u32[]{:S(2)}) %collective-permute-start.13) | collective-permute-done | bytes 131104 | tf_op jit(solution)/shard_map/ppermute | solution.py:38
  132.2 1.3 copy.10
  133.6 1.0 copy.12
  134.6 0.7 dynamic-slice_multiply_fusion
  135.3 5.4 %collective-permute-done.14 = bf16[128,512]{1,0:T(8,128)(2,1)S(1)} collective-permute-done((bf16[128,512]{1,0:T(8,128)(2,1)S(1)}, bf16[128,512]{1,0:T(8,128)(2,1)S(1)}, u32[]{:S(2)}, u32[]{:S(2)}) %collective-permute-start.14) | collective-permute-done | bytes 131104 | tf_op jit(solution)/shard_map/ppermute | solution.py:38
  141.3 1.5 constant_dynamic-slice_fusion.3
  142.8 2.5 %reshape.58 = bf16[2,1024,4,128]{3,2,1,0:T(4,128)(2,1)S(1)} reshape(bf16[2048,512]{1,0:T(8,128)(2,1)} %constant_dynamic-slice_fusion.3) | data formatting | bytes 4194304 | tf_op jit(solution)/shard_map/reshape | solution.py:51
  145.4 31.1 %all-gather.2.cloned.1.call-done = bf16[2048,512]{1,0:T(8,128)(2,1)} async-done(((bf16[128,512]{1,0:T(8,128)(2,1)}), bf16[2048,512]{1,0:T(8,128)(2,1)}) %all-gather.2.cloned.1.call-update) | async-done | bytes 2097168 | tf_op jit(solution)/shard_map/all_gather | solution.py:30
  176.4 4.0 %reshape.56 = bf16[2,1024,4,128]{3,2,1,0:T(4,128)(2,1)} reshape(bf16[2048,512]{1,0:T(8,128)(2,1)} %all-gather.2.cloned.1.call-done) | data formatting | bytes 4194304 | tf_op jit(solution)/shard_map/reshape | solution.py:50
  180.4 34.2 %while.15 = (s32[]{:T(128)}, f32[4,4,128]{2,1,0:T(4,128)S(1)}, f32[4,4,128]{2,1,0:T(4,128)S(1)}, f32[4,4,128,128]{3,2,1,0:T(8,128)}, s32[2,1024]{1,0:T(2,128)S(1...) while((s32[]{:T(128)}, f32[4,4,128]{2,1,0:T(4,128)S(1)}, ...), condition=%wide.region_3.4_spmd.clone, body=%wide.region_0.3_spmd.clone.sunk | while | flops 1101932672 | bytes 70400192 | solution.py:74
  180.5 0.1 le.33
  180.6 0.2 broadcast_compare_fusion.2
  180.8 2.0 constant_dynamic-slice_fusion.7
  182.8 4.6 %fusion.30 = (f32[4,4,128]{2,1,0:T(4,128)S(1)}, f32[4,1024,128,4]{2,1,3,0:T(8,128)}) fusion(pred[128,1024]{0,1:T(8,128)(4,1)S(1)} %broadcast_compare_fusion.2, bf16[128,4,4,128]{3,0,2,1:T(8,128)(2,1)S(1)} %copy-done.1, bf16[1,1024,4,128]{3,2,1,0:T(4,128)(2,1)S(1)} %get-tuple-element.182), kind=kOutput, calls=%fused_computation.3.clone.1 | convolution fusion | flops 543160320 | bytes 10100736 | tf_op jit(solution)/shard_map/while/body/eval_jaxpr/qhgd,khd->hgqk/dot_general | solution.py:57
  187.4 4.6 %fusion.31 = f32[4,4,128]{2,1,0:T(4,128)S(1)} fusion(f32[4,1024,128,4]{2,1,3,0:T(8,128)} %get-tuple-element.184, f32[4,4,128]{2,1,0:T(4,128)S(1)} %select_maximum_fusion.2, pred[128,1024]{0,1:T(8,128)(4,1)S(1)} %broadcast_compare_fusion.2), kind=kLoop, calls=%fused_computation.5.clone.1 | loop fusion | flops 10483712 | bytes 8536064 | tf_op jit(solution)/shard_map/while/body/eval_jaxpr/reduce_sum | solution.py:65
  192.0 1.2 copy-done
  193.2 3.8 %fusion.33 = f32[4,4,128,128]{3,2,1,0:T(8,128)} fusion(f32[4,1024,128,4]{2,1,3,0:T(8,128)S(1)} %copy-done, f32[4,4,128]{2,1,0:T(4,128)S(1)} %select_maximum_fusion.2, pred[128,1024]{0,1:T(8,128)(4,1)S(1)} %broadcast_compare_fusion.2, bf16[1,1024,4,128]{3,2,1,0:T(4,128)(2,1)S(1)} %get-tuple-element.186, f32[4,4,128,128]{3,2,1,0:T(8,128)} %get-tuple-element.202, ...), kind=kOutput, calls=%fused_computation.8.clone.1 | convolution fusion | flops 548143104 | bytes 11681793 | tf_op jit(solution)/shard_map/while/body/eval_jaxpr/hgqk,khd->hgqd/dot_general | solution.py:66
  197.1 0.1 le.33
  197.2 0.2 broadcast_compare_fusion.2
  197.4 2.0 constant_dynamic-slice_fusion.7
  199.4 4.6 %fusion.30 = (f32[4,4,128]{2,1,0:T(4,128)S(1)}, f32[4,1024,128,4]{2,1,3,0:T(8,128)}) fusion(pred[128,1024]{0,1:T(8,128)(4,1)S(1)} %broadcast_compare_fusion.2, bf16[128,4,4,128]{3,0,2,1:T(8,128)(2,1)S(1)} %copy-done.1, bf16[1,1024,4,128]{3,2,1,0:T(4,128)(2,1)S(1)} %get-tuple-element.182), kind=kOutput, calls=%fused_computation.3.clone.1 | convolution fusion | flops 543160320 | bytes 10100736 | tf_op jit(solution)/shard_map/while/body/eval_jaxpr/qhgd,khd->hgqk/dot_general | solution.py:57
  204.0 4.6 %fusion.31 = f32[4,4,128]{2,1,0:T(4,128)S(1)} fusion(f32[4,1024,128,4]{2,1,3,0:T(8,128)} %get-tuple-element.184, f32[4,4,128]{2,1,0:T(4,128)S(1)} %select_maximum_fusion.2, pred[128,1024]{0,1:T(8,128)(4,1)S(1)} %broadcast_compare_fusion.2), kind=kLoop, calls=%fused_computation.5.clone.1 | loop fusion | flops 10483712 | bytes 8536064 | tf_op jit(solution)/shard_map/while/body/eval_jaxpr/reduce_sum | solution.py:65
  208.6 1.2 copy-done
  209.8 4.8 %fusion.33 = f32[4,4,128,128]{3,2,1,0:T(8,128)} fusion(f32[4,1024,128,4]{2,1,3,0:T(8,128)S(1)} %copy-done, f32[4,4,128]{2,1,0:T(4,128)S(1)} %select_maximum_fusion.2, pred[128,1024]{0,1:T(8,128)(4,1)S(1)} %broadcast_compare_fusion.2, bf16[1,1024,4,128]{3,2,1,0:T(4,128)(2,1)S(1)} %get-tuple-element.186, f32[4,4,128,128]{3,2,1,0:T(8,128)} %get-tuple-element.202, ...), kind=kOutput, calls=%fused_computation.8.clone.1 | convolution fusion | flops 548143104 | bytes 11681793 | tf_op jit(solution)/shard_map/while/body/eval_jaxpr/hgqk,khd->hgqd/dot_general | solution.py:66
  214.6 1.6 copy.14
  216.2 0.1 divide_convert_fusion
  216.4 9.2 %convolution_convert_fusion = bf16[128,4096]{1,0:T(8,128)(2,1)} fusion(bf16[128,2048]{0,1:T(8,128)(2,1)S(1)} %bitcast.49, bf16[2048,4096]{1,0:T(8,128)(2,1)} %param.12), kind=kOutput, calls=%fused_computation.25 | convolution fusion | flops 2148007936 | bytes 18350080 | tf_op jit(solution)/shard_map/dot_general | solution.py:82
  225.6 7.3 %reduce-scatter.2.cloned.1.call-done = bf16[128,2048]{1,0:T(8,128)(2,1)} async-done(((bf16[128,4096]{1,0:T(8,128)(2,1)}), bf16[128,2048]{1,0:T(8,128)(2,1)}) %reduce-scatter.2.cloned.1.call-update) | async-done | bytes 524304 | tf_op jit(solution)/shard_map/reduce_scatter | solution.py:83
  232.9 1.3 fusion.16
  234.2 2.5 %psum.7 = f32[128]{0:T(128)S(1)} all-reduce(f32[128]{0:T(128)S(1)} %fusion.16), channel_id=1, replica_groups=mesh['ctx'=16,'tp'=2] {'tp'}, use_global_device_ids=true, to_apply=%region_6.7 | all-reduce | flops 128 | bytes 1024 | tf_op jit(solution)/shard_map/psum | solution.py:88
  236.7 2.0 fusion.18
  (81 shorter events, 0.9 us)
Async XLA Ops:
  6.5 134.5 %copy-start.3 = (bf16[128,512]{1,0:T(8,128)(2,1)S(1)}, bf16[128,512]{1,0:T(8,128)(2,1)}, u32[]{:S(2)}) copy-start(bf16[128,512]{1,0:T(8,128)(2,1)} %param.11) | copy-start | bytes 393220
  6.5 169.9 %all-gather.2.cloned.1.call-start = ((), (), s32[]{:S(2)}) async-start(), calls=%async_computation.1 | async-start | bytes 2228224 | tf_op jit(solution)/shard_map/all_gather | solution.py:30
  6.5 10.7 %collective-permute-start = (bf16[128,512]{1,0:T(8,128)(2,1)}, bf16[128,512]{1,0:T(8,128)(2,1)S(1)}, u32[]{:S(2)}, u32[]{:S(2)}) collective-permute-start(bf16[128,512]{1,0:T(8,128)(2,1)} %param.11), channel_id=1, source_target_pairs={{0,2},{2,4},{4,6},{6,8},{8,10},{10,12},{12,14},{14,16},{16,18},{18... | collective-permute-start | bytes 393224 | tf_op jit(solution)/shard_map/ppermute | solution.py:38
  17.3 8.6 %collective-permute-start.1 = (bf16[128,512]{1,0:T(8,128)(2,1)S(1)}, bf16[128,512]{1,0:T(8,128)(2,1)S(1)}, u32[]{:S(2)}, u32[]{:S(2)}) collective-permute-start(bf16[128,512]{1,0:T(8,128)(2,1)S(1)} %collective-permute-done), channel_id=1, source_target_pairs={{0,2},{2,4},{4,6},{6,8},{8,10},{10,12},{12,14},{14,16},{16,18},{18... | collective-permute-start | bytes 393224 | tf_op jit(solution)/shard_map/ppermute | solution.py:38
  25.8 8.6 %collective-permute-start.2 = (bf16[128,512]{1,0:T(8,128)(2,1)S(1)}, bf16[128,512]{1,0:T(8,128)(2,1)S(1)}, u32[]{:S(2)}, u32[]{:S(2)}) collective-permute-start(bf16[128,512]{1,0:T(8,128)(2,1)S(1)} %collective-permute-done.1), channel_id=1, source_target_pairs={{0,2},{2,4},{4,6},{6,8},{8,10},{10,12},{12,14},{14,16},{16,18},{18... | collective-permute-start | bytes 393224 | tf_op jit(solution)/shard_map/ppermute | solution.py:38
  34.4 8.6 %collective-permute-start.3 = (bf16[128,512]{1,0:T(8,128)(2,1)S(1)}, bf16[128,512]{1,0:T(8,128)(2,1)S(1)}, u32[]{:S(2)}, u32[]{:S(2)}) collective-permute-start(bf16[128,512]{1,0:T(8,128)(2,1)S(1)} %collective-permute-done.2), channel_id=1, source_target_pairs={{0,2},{2,4},{4,6},{6,8},{8,10},{10,12},{12,14},{14,16},{16,18},{18... | collective-permute-start | bytes 393224 | tf_op jit(solution)/shard_map/ppermute | solution.py:38
  43.0 8.6 %collective-permute-start.4 = (bf16[128,512]{1,0:T(8,128)(2,1)S(1)}, bf16[128,512]{1,0:T(8,128)(2,1)S(1)}, u32[]{:S(2)}, u32[]{:S(2)}) collective-permute-start(bf16[128,512]{1,0:T(8,128)(2,1)S(1)} %collective-permute-done.3), channel_id=1, source_target_pairs={{0,2},{2,4},{4,6},{6,8},{8,10},{10,12},{12,14},{14,16},{16,18},{18... | collective-permute-start | bytes 393224 | tf_op jit(solution)/shard_map/ppermute | solution.py:38
  51.5 8.9 %collective-permute-start.5 = (bf16[128,512]{1,0:T(8,128)(2,1)S(1)}, bf16[128,512]{1,0:T(8,128)(2,1)S(1)}, u32[]{:S(2)}, u32[]{:S(2)}) collective-permute-start(bf16[128,512]{1,0:T(8,128)(2,1)S(1)} %collective-permute-done.4), channel_id=1, source_target_pairs={{0,2},{2,4},{4,6},{6,8},{8,10},{10,12},{12,14},{14,16},{16,18},{18... | collective-permute-start | bytes 393224 | tf_op jit(solution)/shard_map/ppermute | solution.py:38
  60.4 9.9 %collective-permute-start.6 = (bf16[128,512]{1,0:T(8,128)(2,1)S(1)}, bf16[128,512]{1,0:T(8,128)(2,1)S(1)}, u32[]{:S(2)}, u32[]{:S(2)}) collective-permute-start(bf16[128,512]{1,0:T(8,128)(2,1)S(1)} %collective-permute-done.5), channel_id=1, source_target_pairs={{0,2},{2,4},{4,6},{6,8},{8,10},{10,12},{12,14},{14,16},{16,18},{18... | collective-permute-start | bytes 393224 | tf_op jit(solution)/shard_map/ppermute | solution.py:38
  70.3 9.1 %collective-permute-start.7 = (bf16[128,512]{1,0:T(8,128)(2,1)S(1)}, bf16[128,512]{1,0:T(8,128)(2,1)S(1)}, u32[]{:S(2)}, u32[]{:S(2)}) collective-permute-start(bf16[128,512]{1,0:T(8,128)(2,1)S(1)} %collective-permute-done.6), channel_id=1, source_target_pairs={{0,2},{2,4},{4,6},{6,8},{8,10},{10,12},{12,14},{14,16},{16,18},{18... | collective-permute-start | bytes 393224 | tf_op jit(solution)/shard_map/ppermute | solution.py:38
  79.4 8.6 %collective-permute-start.8 = (bf16[128,512]{1,0:T(8,128)(2,1)S(1)}, bf16[128,512]{1,0:T(8,128)(2,1)S(1)}, u32[]{:S(2)}, u32[]{:S(2)}) collective-permute-start(bf16[128,512]{1,0:T(8,128)(2,1)S(1)} %collective-permute-done.7), channel_id=1, source_target_pairs={{0,2},{2,4},{4,6},{6,8},{8,10},{10,12},{12,14},{14,16},{16,18},{18... | collective-permute-start | bytes 393224 | tf_op jit(solution)/shard_map/ppermute | solution.py:38
  88.0 8.6 %collective-permute-start.9 = (bf16[128,512]{1,0:T(8,128)(2,1)S(1)}, bf16[128,512]{1,0:T(8,128)(2,1)S(1)}, u32[]{:S(2)}, u32[]{:S(2)}) collective-permute-start(bf16[128,512]{1,0:T(8,128)(2,1)S(1)} %collective-permute-done.8), channel_id=1, source_target_pairs={{0,2},{2,4},{4,6},{6,8},{8,10},{10,12},{12,14},{14,16},{16,18},{18... | collective-permute-start | bytes 393224 | tf_op jit(solution)/shard_map/ppermute | solution.py:38
  96.5 8.6 %collective-permute-start.10 = (bf16[128,512]{1,0:T(8,128)(2,1)S(1)}, bf16[128,512]{1,0:T(8,128)(2,1)S(1)}, u32[]{:S(2)}, u32[]{:S(2)}) collective-permute-start(bf16[128,512]{1,0:T(8,128)(2,1)S(1)} %collective-permute-done.9), channel_id=1, source_target_pairs={{0,2},{2,4},{4,6},{6,8},{8,10},{10,12},{12,14},{14,16},{16,18},{18... | collective-permute-start | bytes 393224 | tf_op jit(solution)/shard_map/ppermute | solution.py:38
  105.1 8.6 %collective-permute-start.11 = (bf16[128,512]{1,0:T(8,128)(2,1)S(1)}, bf16[128,512]{1,0:T(8,128)(2,1)S(1)}, u32[]{:S(2)}, u32[]{:S(2)}) collective-permute-start(bf16[128,512]{1,0:T(8,128)(2,1)S(1)} %collective-permute-done.10), channel_id=1, source_target_pairs={{0,2},{2,4},{4,6},{6,8},{8,10},{10,12},{12,14},{14,16},{16,18},{18... | collective-permute-start | bytes 393224 | tf_op jit(solution)/shard_map/ppermute | solution.py:38
  113.6 8.9 %collective-permute-start.12 = (bf16[128,512]{1,0:T(8,128)(2,1)S(1)}, bf16[128,512]{1,0:T(8,128)(2,1)S(1)}, u32[]{:S(2)}, u32[]{:S(2)}) collective-permute-start(bf16[128,512]{1,0:T(8,128)(2,1)S(1)} %collective-permute-done.11), channel_id=1, source_target_pairs={{0,2},{2,4},{4,6},{6,8},{8,10},{10,12},{12,14},{14,16},{16,18},{18... | collective-permute-start | bytes 393224 | tf_op jit(solution)/shard_map/ppermute | solution.py:38
  113.7 119.3 %reduce-scatter.2.cloned.1.call-start = ((), (), s32[]{:S(2)}) async-start(), calls=%async_computation.2 | async-start | bytes 1572864 | tf_op jit(solution)/shard_map/reduce_scatter | solution.py:83
  122.5 9.6 %collective-permute-start.13 = (bf16[128,512]{1,0:T(8,128)(2,1)S(1)}, bf16[128,512]{1,0:T(8,128)(2,1)S(1)}, u32[]{:S(2)}, u32[]{:S(2)}) collective-permute-start(bf16[128,512]{1,0:T(8,128)(2,1)S(1)} %collective-permute-done.12), channel_id=1, source_target_pairs={{0,2},{2,4},{4,6},{6,8},{8,10},{10,12},{12,14},{14,16},{16,18},{18... | collective-permute-start | bytes 393224 | tf_op jit(solution)/shard_map/ppermute | solution.py:38
  132.2 8.6 %collective-permute-start.14 = (bf16[128,512]{1,0:T(8,128)(2,1)S(1)}, bf16[128,512]{1,0:T(8,128)(2,1)S(1)}, u32[]{:S(2)}, u32[]{:S(2)}) collective-permute-start(bf16[128,512]{1,0:T(8,128)(2,1)S(1)} %collective-permute-done.13), channel_id=1, source_target_pairs={{0,2},{2,4},{4,6},{6,8},{8,10},{10,12},{12,14},{14,16},{16,18},{18... | collective-permute-start | bytes 393224 | tf_op jit(solution)/shard_map/ppermute | solution.py:38
  180.6 2.2 copy-start.1
  187.4 5.8 %copy-start = (f32[4,1024,128,4]{2,1,3,0:T(8,128)S(1)}, f32[4,1024,128,4]{2,1,3,0:T(8,128)}, u32[]{:S(2)}) copy-start(f32[4,1024,128,4]{2,1,3,0:T(8,128)} %get-tuple-element.184) | copy-start | bytes 25165828 | tf_op jit(solution)/shard_map/while
  197.2 2.2 copy-start.1
  204.0 5.8 %copy-start = (f32[4,1024,128,4]{2,1,3,0:T(8,128)S(1)}, f32[4,1024,128,4]{2,1,3,0:T(8,128)}, u32[]{:S(2)}) copy-start(f32[4,1024,128,4]{2,1,3,0:T(8,128)} %get-tuple-element.184) | copy-start | bytes 25165828 | tf_op jit(solution)/shard_map/while
  216.3 9.2 %copy-start.4 = (bf16[2048]{0:T(1024)(128)(2,1)S(1)}, bf16[2048]{0:T(1024)(128)(2,1)}, u32[]{:S(2)}) copy-start(bf16[2048]{0:T(1024)(128)(2,1)} %param.14) | copy-start | bytes 12292
  216.3 16.6 %copy-start.2 = (bf16[128,2048]{1,0:T(8,128)(2,1)S(1)}, bf16[128,2048]{1,0:T(8,128)(2,1)}, u32[]{:S(2)}) copy-start(bf16[128,2048]{1,0:T(8,128)(2,1)} %param.13) | copy-start | bytes 1572868
Sparse Core Ops, SparseCore 0:
  113.8 62.5 all-gather.1
  225.7 7.1 reduce-scatter.1
